TPU v7x, 32 devices: a whole 2x2x4 slice. The times are simulated.
32 devices in a mesh: rep: 4 (over y, x), shard: 8 (over z, core).
Axes of the slice: x: 2, y: 2, z: 4, core: 2. Of those that a mesh axis runs over, the one named last changes fastest.
Arguments:
- inputs: bfloat16 [4, 1792, 768], P('rep', 'shard'), may hold values from -6 to 6
- cotangent: bfloat16 [4, 1792, 768], P('rep', 'shard'), may hold values from -6 to 6
- lengths: int32 [4], P('rep'), may hold values from 448 to 1792, as said below
- w_query: bfloat16 [768, 768], P('shard'), may hold values from -0.3125 to 0.3125
- w_key: bfloat16 [768, 768], P('shard'), may hold values from -0.3125 to 0.3125
- w_value: bfloat16 [768, 768], P('shard'), may hold values from -0.21875 to 0.21875
- w_out: bfloat16 [768, 768], P('shard'), may hold values from -1.25 to 1.25
- b_query: bfloat16 [768], P('shard'), may hold values from -1.5 to 1.5
- b_value: bfloat16 [768], P('shard'), may hold values from -0.25 to 0.25
- b_out: bfloat16 [768], P('shard'), may hold values from -1.5 to 1.5
- gain_one: bfloat16 [768], P('shard'), may hold values from 0.5 to 1.5
- shift_one: bfloat16 [768], P('shard'), may hold values from -1.5 to 1.5
- w_up: bfloat16 [768, 3072], P('shard'), may hold values from -0.21875 to 0.21875
- b_up: bfloat16 [3072], P('shard'), may hold values from -1.5 to 1.5
- w_down: bfloat16 [3072, 768], P('shard'), may hold values from -0.15625 to 0.15625
- b_down: bfloat16 [768], P('shard'), may hold values from -1.5 to 1.5
- gain_two: bfloat16 [768], P('shard'), may hold values from 0.5 to 1.5
- shift_two: bfloat16 [768], P('shard'), may hold values from -1.5 to 1.5
Outputs:
- layer_output: bfloat16 [4, 1792, 768], P('rep', 'shard')
- input_grad: float32 [4, 1792, 768], P('rep', 'shard')
- grad_w_query: float32 [768, 768], P('shard')
- grad_w_key: float32 [768, 768], P('shard')
- grad_w_value: float32 [768, 768], P('shard')
- grad_w_out: float32 [768, 768], P('shard')
- grad_b_query: float32 [768], P('shard')
- grad_b_value: float32 [768], P('shard')
- grad_b_out: float32 [768], P('shard')
- grad_gain_one: float32 [768], P('shard')
- grad_shift_one: float32 [768], P('shard')
- grad_w_up: float32 [768, 3072], P('shard')
- grad_b_up: float32 [3072], P('shard')
- grad_w_down: float32 [3072, 768], P('shard')
- grad_b_down: float32 [768], P('shard')
- grad_gain_two: float32 [768], P('shard')
- grad_shift_two: float32 [768], P('shard')
Inputs may be any that keep to these rules, and one draw needn't show every extreme that they name: `lengths`: slot 0 is full; the others hold between a quarter of 1792 and 1792 valid tokens.
All inputs are finite; a program needn't handle non-finite values.
Results may differ from a plain program's by a relative error of at most 0.024.
Values may be sent and summed in bfloat16 or wider, within the bound.
No kernel may reach another device: no remote copies, remote signals or barrier semaphores. Data moves between devices by JAX's collectives and lax.ppermute only.
A program may use at most 256 MiB of HBM per device.

v0:
```python
import math
import jax
import jax.numpy as jnp
from jax import lax
from jax.sharding import PartitionSpec as P

HEADS = 12
HEAD_DIM = 64
epsilon = 1e-05
floor_value = -1e30


def inner_rows(left, right):
    return lax.dot_general(
        left, right, (((0,), (0,)), ((), ())), preferred_element_type=jnp.float32
    )


def times_transposed(left, right):
    return lax.dot_general(
        left, right, (((1,), (1,)), ((), ())), preferred_element_type=jnp.float32
    )


def plain_product(left, right):
    return jnp.dot(left, right, preferred_element_type=jnp.float32)


def norm_forward(hidden, gain, shift):
    center = hidden - jnp.mean(hidden, axis=1, keepdims=True)
    inverse = lax.rsqrt(jnp.mean(center * center, axis=1, keepdims=True) + epsilon)
    scaled = center * inverse
    return (scaled * gain.astype(jnp.float32) + shift.astype(jnp.float32), scaled, inverse)


def norm_backward(grad_out, gain, scaled, inverse):
    grad_scaled = grad_out * gain.astype(jnp.float32)
    grad_in = inverse * (
        grad_scaled
        - jnp.mean(grad_scaled, axis=1, keepdims=True)
        - scaled * jnp.mean(grad_scaled * scaled, axis=1, keepdims=True)
    )
    return (grad_in, jnp.sum(grad_out * scaled, axis=0), jnp.sum(grad_out, axis=0))


def gelu_both(upward):
    cumulative = 0.5 * (1.0 + lax.erf(upward * 0.7071067811865476))
    density = jnp.exp(-0.5 * upward * upward) * 0.3989422804014327
    return (upward * cumulative, cumulative + upward * density)


def split_heads(rows):
    return rows.reshape(rows.shape[0], HEADS, HEAD_DIM)


def column_sum(values_low):
    return jnp.sum(values_low.astype(jnp.float32), axis=0)


def body(
    inputs,
    cotangent,
    lengths,
    w_query,
    w_key,
    w_value,
    w_out,
    b_query,
    b_value,
    b_out,
    gain_one,
    shift_one,
    w_up,
    b_up,
    w_down,
    b_down,
    gain_two,
    shift_two,
):
    gathered = (
        lax.all_gather(w_query, "shard", axis=0, tiled=True),
        lax.all_gather(w_key, "shard", axis=0, tiled=True),
        lax.all_gather(w_value, "shard", axis=0, tiled=True),
        lax.all_gather(w_out, "shard", axis=0, tiled=True),
        lax.all_gather(b_query, "shard", axis=0, tiled=True),
        lax.all_gather(b_value, "shard", axis=0, tiled=True),
        lax.all_gather(b_out, "shard", axis=0, tiled=True),
        lax.all_gather(gain_one, "shard", axis=0, tiled=True),
        lax.all_gather(shift_one, "shard", axis=0, tiled=True),
        lax.all_gather(w_up, "shard", axis=0, tiled=True),
        lax.all_gather(b_up, "shard", axis=0, tiled=True),
        lax.all_gather(w_down, "shard", axis=0, tiled=True),
        lax.all_gather(b_down, "shard", axis=0, tiled=True),
        lax.all_gather(gain_two, "shard", axis=0, tiled=True),
        lax.all_gather(shift_two, "shard", axis=0, tiled=True),
    )
    (
        query_full,
        key_full,
        value_full,
        out_full,
        bias_query,
        bias_value,
        bias_out,
        gain_first,
        shift_first,
        up_full,
        bias_up,
        down_full,
        bias_down,
        gain_second,
        shift_second,
    ) = gathered
    tokens = inputs[0]
    rows = tokens.shape[0]
    model = tokens.shape[1]
    scale = HEAD_DIM ** (-0.5)
    length = lengths[0]
    positions = lax.axis_index("shard") * rows + jnp.arange(rows, dtype=jnp.int32)
    own_valid = positions < length
    row_valid = own_valid.astype(jnp.float32)
    source = tokens.astype(jnp.float32)
    query = (plain_product(tokens, query_full) + bias_query.astype(jnp.float32)).astype(
        jnp.bfloat16
    )
    keys = plain_product(tokens, key_full).astype(jnp.bfloat16)
    values = (plain_product(tokens, value_full) + bias_value.astype(jnp.float32)).astype(
        jnp.bfloat16
    )
    pairs = lax.all_gather(jnp.concatenate([keys, values], axis=1), "shard", axis=0, tiled=True)
    total = pairs.shape[0]
    block = math.gcd(total, 1024)
    count = total // block
    query_heads = split_heads(query)

    def block_scores(index):
        start = index * block
        piece = lax.dynamic_slice_in_dim(pairs, start, block, 0)
        key_heads = split_heads(piece[:, :model])
        value_heads = split_heads(piece[:, model:])
        scores = (
            jnp.einsum("qhd,khd->hqk", query_heads, key_heads, preferred_element_type=jnp.float32)
            * scale
        )
        key_valid = start + jnp.arange(block, dtype=jnp.int32) < length
        return (scores, key_valid[None, None, :], key_heads, value_heads)

    def running_max(index, carry):
        highest, summed = carry
        scores, key_valid, key_heads, value_heads = block_scores(index)
        masked = jnp.where(key_valid, scores, floor_value)
        newest = jnp.maximum(highest, jnp.max(masked, axis=2))
        weights = jnp.where(key_valid, jnp.exp(masked - newest[:, :, None]), 0.0)
        return (newest, summed * jnp.exp(highest - newest) + jnp.sum(weights, axis=2))

    start_max = jnp.full((HEADS, rows), floor_value, jnp.float32)
    highest, summed = lax.fori_loop(
        0, count, running_max, (start_max, jnp.zeros((HEADS, rows), jnp.float32))
    )
    log_total = highest + jnp.log(summed)

    def weighted(index, mixed_sum):
        scores, key_valid, key_heads, value_heads = block_scores(index)
        probs = jnp.where(key_valid, jnp.exp(scores - log_total[:, :, None]), 0.0).astype(
            jnp.bfloat16
        )
        return mixed_sum + jnp.einsum(
            "hqk,khd->qhd", probs, value_heads, preferred_element_type=jnp.float32
        )

    mixed = lax.fori_loop(0, count, weighted, jnp.zeros((rows, HEADS, HEAD_DIM), jnp.float32))
    mixed_low = mixed.reshape(rows, model).astype(jnp.bfloat16)
    branch = plain_product(mixed_low, out_full) + bias_out.astype(jnp.float32)
    normed, scaled_one, inverse_one = norm_forward(source + branch, gain_first, shift_first)
    normed_low = normed.astype(jnp.bfloat16)
    upward = plain_product(normed_low, up_full) + bias_up.astype(jnp.float32)
    active, slope = gelu_both(upward)
    active_low = active.astype(jnp.bfloat16)
    second = plain_product(active_low, down_full) + bias_down.astype(jnp.float32)
    result, scaled_two, inverse_two = norm_forward(normed + second, gain_second, shift_second)
    backward_params = (
        lax.all_gather(w_query, "shard", axis=0, tiled=True),
        lax.all_gather(w_key, "shard", axis=0, tiled=True),
        lax.all_gather(w_value, "shard", axis=0, tiled=True),
        lax.all_gather(w_out, "shard", axis=0, tiled=True),
        lax.all_gather(b_query, "shard", axis=0, tiled=True),
        lax.all_gather(b_value, "shard", axis=0, tiled=True),
        lax.all_gather(b_out, "shard", axis=0, tiled=True),
        lax.all_gather(gain_one, "shard", axis=0, tiled=True),
        lax.all_gather(shift_one, "shard", axis=0, tiled=True),
        lax.all_gather(w_up, "shard", axis=0, tiled=True),
        lax.all_gather(b_up, "shard", axis=0, tiled=True),
        lax.all_gather(w_down, "shard", axis=0, tiled=True),
        lax.all_gather(b_down, "shard", axis=0, tiled=True),
        lax.all_gather(gain_two, "shard", axis=0, tiled=True),
        lax.all_gather(shift_two, "shard", axis=0, tiled=True),
    )
    query_back = backward_params[0]
    key_back = backward_params[1]
    value_back = backward_params[2]
    out_back = backward_params[3]
    gain_first_back = backward_params[7]
    up_back = backward_params[9]
    down_back = backward_params[11]
    gain_second_back = backward_params[13]
    grad_result = cotangent[0].astype(jnp.float32) * row_valid[:, None]
    grad_sum_two, grad_gain_second, grad_shift_second = norm_backward(
        grad_result, gain_second_back, scaled_two, inverse_two
    )
    grad_second = grad_sum_two.astype(jnp.bfloat16)
    grad_down = inner_rows(active_low, grad_second)
    grad_bias_down = column_sum(grad_second)
    grad_upward = (times_transposed(grad_second, down_back) * slope).astype(jnp.bfloat16)
    grad_up = inner_rows(normed_low, grad_upward)
    grad_bias_up = column_sum(grad_upward)
    grad_normed = grad_sum_two + times_transposed(grad_upward, up_back)
    grad_sum_one, grad_gain_first, grad_shift_first = norm_backward(
        grad_normed, gain_first_back, scaled_one, inverse_one
    )
    grad_branch = grad_sum_one.astype(jnp.bfloat16)
    grad_out_proj = inner_rows(mixed_low, grad_branch)
    grad_bias_out = column_sum(grad_branch)
    grad_mixed = times_transposed(grad_branch, out_back).astype(jnp.bfloat16)
    grad_mixed_heads = split_heads(grad_mixed)
    delta = jnp.einsum("qhd,qhd->hq", grad_mixed_heads.astype(jnp.float32), mixed)

    def key_grads(index, carry):
        grad_query_sum, buffer = carry
        scores, key_valid, key_heads, value_heads = block_scores(index)
        probs = jnp.where(key_valid, jnp.exp(scores - log_total[:, :, None]), 0.0)
        probs_low = probs.astype(jnp.bfloat16)
        grad_probs = jnp.einsum(
            "qhd,khd->hqk", grad_mixed_heads, value_heads, preferred_element_type=jnp.float32
        )
        grad_scores = (probs * (grad_probs - delta[:, :, None])).astype(jnp.bfloat16)
        grad_query_sum = (
            grad_query_sum
            + jnp.einsum("hqk,khd->qhd", grad_scores, key_heads, preferred_element_type=jnp.float32)
            * scale
        )
        key_part = (
            jnp.einsum("hqk,qhd->khd", grad_scores, query_heads, preferred_element_type=jnp.float32)
            * scale
        )
        value_part = jnp.einsum(
            "hqk,qhd->khd", probs_low, grad_mixed_heads, preferred_element_type=jnp.float32
        )
        update = jnp.concatenate(
            [key_part.reshape(block, model), value_part.reshape(block, model)], axis=1
        )
        buffer = lax.dynamic_update_slice_in_dim(buffer, update, index * block, 0)
        return (grad_query_sum, buffer)

    grad_query_sum, buffer = lax.fori_loop(
        0,
        count,
        key_grads,
        (
            jnp.zeros((rows, HEADS, HEAD_DIM), jnp.float32),
            jnp.zeros((total, 2 * model), jnp.float32),
        ),
    )
    grad_pairs = lax.psum_scatter(
        buffer.astype(jnp.bfloat16), "shard", scatter_dimension=0, tiled=True
    ).astype(jnp.float32)
    grad_query = grad_query_sum.reshape(rows, model)
    grad_keys = grad_pairs[:, :model]
    grad_values = grad_pairs[:, model:]
    query_low = grad_query.astype(jnp.bfloat16)
    keys_low = grad_keys.astype(jnp.bfloat16)
    values_low = grad_values.astype(jnp.bfloat16)
    grad_query_proj = inner_rows(tokens, query_low)
    grad_key_proj = inner_rows(tokens, keys_low)
    grad_value_proj = inner_rows(tokens, values_low)
    grad_bias_query = column_sum(query_low)
    grad_bias_value = column_sum(values_low)
    grad_input = (
        grad_sum_one
        + times_transposed(query_low, query_back)
        + times_transposed(keys_low, key_back)
        + times_transposed(values_low, value_back)
    )
    shared = (
        lax.psum_scatter(
            grad_query_proj.astype(jnp.bfloat16), "shard", scatter_dimension=0, tiled=True
        ).astype(jnp.float32),
        lax.psum_scatter(
            grad_key_proj.astype(jnp.bfloat16), "shard", scatter_dimension=0, tiled=True
        ).astype(jnp.float32),
        lax.psum_scatter(
            grad_value_proj.astype(jnp.bfloat16), "shard", scatter_dimension=0, tiled=True
        ).astype(jnp.float32),
        lax.psum_scatter(
            grad_out_proj.astype(jnp.bfloat16), "shard", scatter_dimension=0, tiled=True
        ).astype(jnp.float32),
        lax.psum_scatter(
            grad_bias_query.astype(jnp.bfloat16), "shard", scatter_dimension=0, tiled=True
        ).astype(jnp.float32),
        lax.psum_scatter(
            grad_bias_value.astype(jnp.bfloat16), "shard", scatter_dimension=0, tiled=True
        ).astype(jnp.float32),
        lax.psum_scatter(
            grad_bias_out.astype(jnp.bfloat16), "shard", scatter_dimension=0, tiled=True
        ).astype(jnp.float32),
        lax.psum_scatter(
            grad_gain_first.astype(jnp.bfloat16), "shard", scatter_dimension=0, tiled=True
        ).astype(jnp.float32),
        lax.psum_scatter(
            grad_shift_first.astype(jnp.bfloat16), "shard", scatter_dimension=0, tiled=True
        ).astype(jnp.float32),
        lax.psum_scatter(
            grad_up.astype(jnp.bfloat16), "shard", scatter_dimension=0, tiled=True
        ).astype(jnp.float32),
        lax.psum_scatter(
            grad_bias_up.astype(jnp.bfloat16), "shard", scatter_dimension=0, tiled=True
        ).astype(jnp.float32),
        lax.psum_scatter(
            grad_down.astype(jnp.bfloat16), "shard", scatter_dimension=0, tiled=True
        ).astype(jnp.float32),
        lax.psum_scatter(
            grad_bias_down.astype(jnp.bfloat16), "shard", scatter_dimension=0, tiled=True
        ).astype(jnp.float32),
        lax.psum_scatter(
            grad_gain_second.astype(jnp.bfloat16), "shard", scatter_dimension=0, tiled=True
        ).astype(jnp.float32),
        lax.psum_scatter(
            grad_shift_second.astype(jnp.bfloat16), "shard", scatter_dimension=0, tiled=True
        ).astype(jnp.float32),
    )
    (
        part_query,
        part_key,
        part_value,
        part_out,
        part_bias_query,
        part_bias_value,
        part_bias_out,
        part_gain_first,
        part_shift_first,
        part_up,
        part_bias_up,
        part_down,
        part_bias_down,
        part_gain_second,
        part_shift_second,
    ) = shared
    summed = (
        lax.psum(part_query.astype(jnp.bfloat16), "rep").astype(jnp.float32),
        lax.psum(part_key.astype(jnp.bfloat16), "rep").astype(jnp.float32),
        lax.psum(part_value.astype(jnp.bfloat16), "rep").astype(jnp.float32),
        lax.psum(part_out.astype(jnp.bfloat16), "rep").astype(jnp.float32),
        lax.psum(part_bias_query.astype(jnp.bfloat16), "rep").astype(jnp.float32),
        lax.psum(part_bias_value.astype(jnp.bfloat16), "rep").astype(jnp.float32),
        lax.psum(part_bias_out.astype(jnp.bfloat16), "rep").astype(jnp.float32),
        lax.psum(part_gain_first.astype(jnp.bfloat16), "rep").astype(jnp.float32),
        lax.psum(part_shift_first.astype(jnp.bfloat16), "rep").astype(jnp.float32),
        lax.psum(part_up.astype(jnp.bfloat16), "rep").astype(jnp.float32),
        lax.psum(part_bias_up.astype(jnp.bfloat16), "rep").astype(jnp.float32),
        lax.psum(part_down.astype(jnp.bfloat16), "rep").astype(jnp.float32),
        lax.psum(part_bias_down.astype(jnp.bfloat16), "rep").astype(jnp.float32),
        lax.psum(part_gain_second.astype(jnp.bfloat16), "rep").astype(jnp.float32),
        lax.psum(part_shift_second.astype(jnp.bfloat16), "rep").astype(jnp.float32),
    )
    return (result.astype(jnp.bfloat16)[None], grad_input[None]) + tuple(summed)


def solution(mesh):
    placed = (
        P("rep", "shard", None),
        P("rep", "shard", None),
        P("rep"),
        P("shard", None),
        P("shard", None),
        P("shard", None),
        P("shard", None),
        P("shard"),
        P("shard"),
        P("shard"),
        P("shard"),
        P("shard"),
        P("shard", None),
        P("shard"),
        P("shard", None),
        P("shard"),
        P("shard"),
        P("shard"),
    )
    return jax.shard_map(
        body,
        mesh=mesh,
        in_specs=placed,
        out_specs=(
            P("rep", "shard", None),
            P("rep", "shard", None),
            P("shard", None),
            P("shard", None),
            P("shard", None),
            P("shard", None),
            P("shard"),
            P("shard"),
            P("shard"),
            P("shard"),
            P("shard"),
            P("shard", None),
            P("shard"),
            P("shard", None),
            P("shard"),
            P("shard"),
            P("shard"),
        ),
        check_vma=False,
    )
```

profile of v0, /device:TPU:0, one launch (start us, length us, event | category | flops | bytes accessed | tf_op | source)
XLA Modules:
  0.0 737.3 jit_solution(4788529265016331617)
XLA Ops:
  17.3 30.8 %all-reduce.18 = (bf16[768]{0:T(1024)(128)(2,1)S(1)}, bf16[768]{0:T(1024)(128)(2,1)S(1)}, bf16[768]{0:T(1024)(128)(2,1)S(1)}, bf16[768]{0:T(1024)(128)(2,1)S(1)}...) all-reduce(bf16[768]{0:T(1024)(128)(2,1)S(1)} %dynamic-update-slice, ...), channel_id=1, replica_groups=mesh['rep'=4,'shard'=8] {'shard'}, use_global_device_ids=true, to_apply=%add | all-reduce | flops 5376 | bytes 21504
  50.0 9.5 %all-gather.11.cloned.1.call-done = bf16[768,768]{1,0:T(8,128)(2,1)} async-done(((bf16[96,768]{1,0:T(8,128)(2,1)}), bf16[768,768]{1,0:T(8,128)(2,1)}) %all-gather.11.cloned.1.call-update) | async-done | bytes 1179664 | tf_op jit(solution)/shard_map/all_gather | solution.py:83
  64.9 13.0 %all-gather = bf16[8,1,384]{2,1,0:T(2,128)(2,1)S(1)} all-gather(bf16[1,1,384]{2,1,0:T(2,128)(2,1)S(1)} %reshape.198), channel_id=1, replica_groups=mesh['rep'=4,'shard'=8] {'shard'}, dimensions={0}, use_global_device_ids=true | all-gather | bytes 6912 | tf_op jit(solution)/shard_map/all_gather | solution.py:91
  78.0 5.5 all-gather.15.cloned.1.call-done
  85.4 58.1 %all-gather.13.cloned.1.call-done = bf16[1792,1536]{1,0:T(8,128)(2,1)} async-done(((bf16[224,1536]{1,0:T(8,128)(2,1)}), bf16[1792,1536]{1,0:T(8,128)(2,1)}) %all-gather.13.cloned.1.call-update) | async-done | bytes 5505040 | tf_op jit(solution)/shard_map/all_gather | solution.py:130
  143.5 8.3 %copy.55 = bf16[1792,1536]{0,1:T(8,128)(2,1)} copy(bf16[1792,1536]{1,0:T(8,128)(2,1)} %all-gather.13.cloned.1.call-done) | data formatting | bytes 11010048
  151.8 25.8 %while.46 = (s32[]{:T(128)}, f32[12,224]{1,0:T(8,128)S(1)}, f32[12,224]{1,0:T(8,128)S(1)}, s32[]{:T(128)}, bf16[1792,1536]{0,1:T(8,128)(2,1)}, /*index=5*/bf16[2...) while((s32[]{:T(128)}, f32[12,224]{1,0:T(8,128)S(1)}, ...), condition=%wide.region_3.4_spmd.clone, body=%wide.region_0.3_spmd.clone.sunk | while | flops 93599368 | bytes 7169458 | solution.py:157
  177.6 34.2 %while.47 = (s32[]{:T(128)}, f32[224,12,64]{0,2,1:T(8,128)}, bf16[1792,1536]{0,1:T(8,128)(2,1)}, s32[]{:T(128)}, bf16[224,12,64]{0,2,1:T(8,128)(2,1)S(1)}, /*ind...) while((s32[]{:T(128)}, f32[224,12,64]{0,2,1:T(8,128)}, ...), condition=%wide.region_5.6_spmd.clone, body=%wide.region_4.5_spmd.clone.sunk | while | flops 179257856 | bytes 4091081 | solution.py:171
  218.9 5.9 multiply_convert_fusion.1
  224.8 45.7 %all-gather.21.cloned.1.call-done = bf16[3072,768]{1,0:T(8,128)(2,1)} async-done(((bf16[384,768]{1,0:T(8,128)(2,1)}), bf16[3072,768]{1,0:T(8,128)(2,1)}) %all-gather.21.cloned.1.call-update) | async-done | bytes 4718608 | tf_op jit(solution)/shard_map/all_gather | solution.py:92
  290.3 44.6 %while.48 = (s32[]{:T(128)}, f32[224,12,64]{0,2,1:T(8,128)S(1)}, bf16[1792,1536]{0,1:T(8,128)(2,1)}, bf16[1792,1536]{0,1:T(8,128)(2,1)}, s32[]{:T(128)}, /*index...) while((s32[]{:T(128)}, f32[224,12,64]{0,2,1:T(8,128)S(1)}, ...), condition=%wide.region_15.16_spmd.clone, body=%wide.region_14.15_spmd.clone.sunk | while | flops 449765888 | bytes 21660160 | solution.py:254
  334.8 8.3 %copy.69 = bf16[1792,1536]{1,0:T(8,128)(2,1)} copy(bf16[1792,1536]{0,1:T(8,128)(2,1)} %get-tuple-element.395) | data formatting | bytes 11010048
  348.1 56.3 %reduce-scatter.22.cloned.1.call-done = bf16[224,1536]{1,0:T(8,128)(2,1)} async-done(((bf16[1792,1536]{1,0:T(8,128)(2,1)}), bf16[224,1536]{1,0:T(8,128)(2,1)}) %reduce-scatter.22.cloned.1.call-update) | async-done | bytes 688144
  416.0 5.0 convolution_convert_fusion.1
  422.4 4.7 convolution_convert_fusion
  427.2 11.5 %reduce-scatter.24.cloned.1.call-done = bf16[96,768]{1,0:T(8,128)(2,1)} async-done(((bf16[768,768]{1,0:T(8,128)(2,1)}), bf16[96,768]{1,0:T(8,128)(2,1)}) %reduce-scatter.24.cloned.1.call-update) | async-done | bytes 147472
  440.4 31.5 %reduce-scatter.28.cloned.1.call-done = bf16[96,768]{1,0:T(8,128)(2,1)} async-done(((bf16[768,768]{1,0:T(8,128)(2,1)}), bf16[96,768]{1,0:T(8,128)(2,1)}) %reduce-scatter.28.cloned.1.call-update) | async-done | bytes 147472
  473.7 31.9 %reduce-scatter.26.cloned.1.call-done = bf16[96,768]{1,0:T(8,128)(2,1)} async-done(((bf16[768,768]{1,0:T(8,128)(2,1)}), bf16[96,768]{1,0:T(8,128)(2,1)}) %reduce-scatter.26.cloned.1.call-update) | async-done | bytes 147472
  507.3 32.0 %reduce-scatter.16.cloned.1.call-done = bf16[96,768]{1,0:T(8,128)(2,1)} async-done(((bf16[768,768]{1,0:T(8,128)(2,1)}), bf16[96,768]{1,0:T(8,128)(2,1)}) %reduce-scatter.16.cloned.1.call-update) | async-done | bytes 147472 | tf_op jit(solution)/shard_map/reduce_scatter | solution.py:293
  539.3 55.5 %reduce-scatter.18.cloned.1.call-done = bf16[96,3072]{1,0:T(8,128)(2,1)} async-done(((bf16[768,3072]{1,0:T(8,128)(2,1)}), bf16[96,3072]{1,0:T(8,128)(2,1)}) %reduce-scatter.18.cloned.1.call-update) | async-done | bytes 589840 | tf_op jit(solution)/shard_map/reduce_scatter | solution.py:311
  594.8 55.5 %reduce-scatter.20.cloned.1.call-done = bf16[384,768]{1,0:T(8,128)(2,1)} async-done(((bf16[3072,768]{1,0:T(8,128)(2,1)}), bf16[384,768]{1,0:T(8,128)(2,1)}) %reduce-scatter.20.cloned.1.call-update) | async-done | bytes 589840 | tf_op jit(solution)/shard_map/reduce_scatter | solution.py:317
  654.9 26.0 %all-reduce.17 = (bf16[768]{0:T(1024)(128)(2,1)S(1)}, bf16[768]{0:T(1024)(128)(2,1)S(1)}, bf16[768]{0:T(1024)(128)(2,1)S(1)}, bf16[768]{0:T(1024)(128)(2,1)S(1)}...) all-reduce(bf16[768]{0:T(1024)(128)(2,1)S(1)} %dynamic-update-slice, ...), channel_id=1, replica_groups=mesh['rep'=4,'shard'=8] {'shard'}, use_global_device_ids=true, to_apply=%add.7 | all-reduce | flops 9984 | bytes 39936
  681.6 10.0 %all-reduce.19 = (bf16[96]{0:T(256)(128)(2,1)S(1)}, bf16[96]{0:T(256)(128)(2,1)S(1)}, bf16[96]{0:T(256)(128)(2,1)S(1)}, bf16[96]{0:T(256)(128)(2,1)S(1)}, bf16[9...) all-reduce(bf16[96]{0:T(256)(128)(2,1)S(1)} %dynamic-slice.9, ...), channel_id=1, replica_groups=mesh['rep'=4,'shard'=8] {'rep'}, use_global_device_ids=true, to_apply=%region_27.28 | all-reduce | flops 1152 | bytes 4608 | tf_op jit(solution)/shard_map/psum | solution.py:352
  700.3 20.3 %all-reduce.23.cloned.1.call-done = (bf16[96,768]{0,1:T(8,128)(2,1)}, bf16[96,768]{0,1:T(8,128)(2,1)}, bf16[96,768]{0,1:T(8,128)(2,1)}, bf16[96,768]{1,0:T(8,128...) async-done(((bf16[96,768]{0,1:T(8,128)(2,1)}, bf16[96,768]{0,1:T(8,128)(2,1)}, bf16[96,768]{0,1:T(8,128)(2,1)}, bf16[96,768]{1,0:T(8,128)(2,1)}, ...) | async-done | bytes 1769488 | tf_op jit(solution)/shard_map/psum | solution.py:348
  (329 shorter events, 194.0 us)
Async XLA Ops:
  7.2 40.9 %all-gather.9.cloned.1.call-start = ((), (), s32[]{:S(2)}) async-start(), calls=%async_computation.7 | async-start | bytes 1327104 | tf_op jit(solution)/shard_map/all_gather | solution.py:82
  7.9 51.5 %all-gather.11.cloned.1.call-start = ((), (), s32[]{:S(2)}) async-start(), calls=%async_computation.8 | async-start | bytes 1327104 | tf_op jit(solution)/shard_map/all_gather | solution.py:83
  8.7 74.8 %all-gather.15.cloned.1.call-start = ((), (), s32[]{:S(2)}) async-start(), calls=%async_computation.10 | async-start | bytes 1327104 | tf_op jit(solution)/shard_map/all_gather | solution.py:81
  9.4 134.1 %all-gather.13.cloned.1.call-start = ((), (), s32[]{:S(2)}) async-start(), calls=%async_computation.9 | async-start | bytes 6193152 | tf_op jit(solution)/shard_map/all_gather | solution.py:130
  62.2 150.9 %all-gather.17.cloned.1.call-start = ((), (), s32[]{:S(2)}) async-start(), calls=%async_computation.11 | async-start | bytes 1327104 | tf_op jit(solution)/shard_map/all_gather | solution.py:84
  62.8 156.2 %all-gather.19.cloned.1.call-start = ((), (), s32[]{:S(2)}) async-start(), calls=%async_computation.12 | async-start | bytes 5308416 | tf_op jit(solution)/shard_map/all_gather | solution.py:90
  63.4 207.2 %all-gather.21.cloned.1.call-start = ((), (), s32[]{:S(2)}) async-start(), calls=%async_computation.13 | async-start | bytes 5308416 | tf_op jit(solution)/shard_map/all_gather | solution.py:92
  64.1 340.3 %reduce-scatter.22.cloned.1.call-start = ((), (), s32[]{:S(2)}) async-start(), calls=%async_computation.17 | async-start | bytes 6193152
  343.2 95.5 %reduce-scatter.24.cloned.1.call-start = ((), (), s32[]{:S(2)}) async-start(), calls=%async_computation.18 | async-start | bytes 1327104
  348.0 123.9 %reduce-scatter.28.cloned.1.call-start = ((), (), s32[]{:S(2)}) async-start(), calls=%async_computation.20 | async-start | bytes 1327104
  409.4 96.2 %reduce-scatter.26.cloned.1.call-start = ((), (), s32[]{:S(2)}) async-start(), calls=%async_computation.19 | async-start | bytes 1327104
  413.4 125.9 %reduce-scatter.16.cloned.1.call-start = ((), (), s32[]{:S(2)}) async-start(), calls=%async_computation.14 | async-start | bytes 1327104 | tf_op jit(solution)/shard_map/reduce_scatter | solution.py:293
  415.9 178.8 %reduce-scatter.18.cloned.1.call-start = ((), (), s32[]{:S(2)}) async-start(), calls=%async_computation.15 | async-start | bytes 5308416 | tf_op jit(solution)/shard_map/reduce_scatter | solution.py:311
  421.1 229.2 %reduce-scatter.20.cloned.1.call-start = ((), (), s32[]{:S(2)}) async-start(), calls=%async_computation.16 | async-start | bytes 5308416 | tf_op jit(solution)/shard_map/reduce_scatter | solution.py:317
  427.1 224.5 %copy-start.22 = (bf16[96]{0:T(256)(128)(2,1)S(1)}, bf16[96]{0:T(256)(128)(2,1)}, u32[]{:S(2)}) copy-start(bf16[96]{0:T(256)(128)(2,1)} %param.41) | copy-start | bytes 580
  427.1 293.4 %all-reduce.23.cloned.1.call-start = ((), (), s32[]{:S(2)}) async-start(), calls=%async_computation.21 | async-start | bytes 3833856 | tf_op jit(solution)/shard_map/psum | solution.py:348
  473.6 181.2 %copy-start.14 = (bf16[768]{0:T(1024)(128)(2,1)S(1)}, bf16[768]{0:T(1024)(128)(2,1)}, u32[]{:S(2)}) copy-start(bf16[768]{0:T(1024)(128)(2,1)} %get-tuple-element.584) | copy-start | bytes 4612
  473.6 181.2 %copy-start.15 = (bf16[768]{0:T(1024)(128)(2,1)S(1)}, bf16[768]{0:T(1024)(128)(2,1)}, u32[]{:S(2)}) copy-start(bf16[768]{0:T(1024)(128)(2,1)} %get-tuple-element.589) | copy-start | bytes 4612
  473.6 181.2 %copy-start.16 = (bf16[768]{0:T(1024)(128)(2,1)S(1)}, bf16[768]{0:T(1024)(128)(2,1)}, u32[]{:S(2)}) copy-start(bf16[768]{0:T(1024)(128)(2,1)} %get-tuple-element.664) | copy-start | bytes 4612
  473.6 181.2 %copy-start.17 = (bf16[768]{0:T(1024)(128)(2,1)S(1)}, bf16[768]{0:T(1024)(128)(2,1)}, u32[]{:S(2)}) copy-start(bf16[768]{0:T(1024)(128)(2,1)} %get-tuple-element.666) | copy-start | bytes 4612
  473.6 181.2 %copy-start.18 = (bf16[3072]{0:T(1024)(128)(2,1)S(1)}, bf16[3072]{0:T(1024)(128)(2,1)}, u32[]{:S(2)}) copy-start(bf16[3072]{0:T(1024)(128)(2,1)} %get-tuple-element.685) | copy-start | bytes 18436
  473.7 181.2 %copy-start.19 = (bf16[768]{0:T(1024)(128)(2,1)S(1)}, bf16[768]{0:T(1024)(128)(2,1)}, u32[]{:S(2)}) copy-start(bf16[768]{0:T(1024)(128)(2,1)} %get-tuple-element.582) | copy-start | bytes 4612
  473.7 181.2 %copy-start.20 = (bf16[768]{0:T(1024)(128)(2,1)S(1)}, bf16[768]{0:T(1024)(128)(2,1)}, u32[]{:S(2)}) copy-start(bf16[768]{0:T(1024)(128)(2,1)} %get-tuple-element.587) | copy-start | bytes 4612
  507.3 189.1 %copy-start.2 = (bf16[768,768]{1,0:T(8,128)(2,1)S(1)}, bf16[768,768]{1,0:T(8,128)(2,1)}, u32[]{:S(2)}) copy-start(bf16[768,768]{1,0:T(8,128)(2,1)} %all-gather.9.cloned.1.call-done) | copy-start | bytes 3538948
  (25 other events, 135.2 us)
Sparse Core Ops, SparseCore 0:
  9.6 25.6 all-gather.8
  36.9 22.4 all-gather.10
  61.1 22.3 all-gather.14
  85.6 57.9 all-gather.12
  145.0 21.5 all-gather.16
  168.1 50.8 all-gather.18
  220.6 49.9 all-gather.20
  343.3 61.0 reduce-scatter.21
  407.2 31.3 reduce-scatter.23
  440.8 31.0 reduce-scatter.27
  474.2 31.2 reduce-scatter.25
  508.2 30.9 reduce-scatter.15
  541.6 53.1 reduce-scatter.17
  596.9 53.3 reduce-scatter.19
  654.6 65.8 all-reduce.22
where the time goes:
time: 740 us; the launch traced here: 737 us
  waiting for transfers between devices  421 us (57%)
  matrix products  97.8 us (13%)
  blocking collectives  79.9 us (11%)
  local copies, waits for them, and re-layouts  73.4 us (10%)
  other arithmetic  46.9 us (6%)
  between operations  17 us (2%)
    unnamed x19, waiting for transfers between devices  135 us
    all_gather x1, waiting for transfers between devices, body(): lax.all_gather(jnp.concatenate([keys, values], axis=1), 'shard', axis=0,...  58.1 us
    unnamed x2, blocking collectives  56.8 us
    reduce_scatter x1, waiting for transfers between devices, body(): lax.psum_scatter(grad_up.astype(jnp.bfloat16), 'shard', scatter_dimension...  55.5 us
    reduce_scatter x1, waiting for transfers between devices, body(): lax.psum_scatter(grad_down.astype(jnp.bfloat16), 'shard', scatter_dimensi...  55.5 us
    all_gather x1, waiting for transfers between devices, body(): lax.all_gather(w_down, 'shard', axis=0, tiled=True)  45.7 us
    unnamed x92, local copies, waits for them, and re-layouts  44.5 us
    reduce_scatter x1, waiting for transfers between devices, body(): lax.psum_scatter(grad_out_proj.astype(jnp.bfloat16), 'shard', scatter_dim...  32 us
  transfers between devices with their start and end apart: 15, of which 13 were waited for; matrix products, arithmetic and copies ran while one was open for 18% of the time, Pallas kernels for 0%

commit v1 on v0

--- a/solution.py
+++ b/solution.py
@@ -345,7 +345,7 @@
         part_shift_second,
     ) = shared
     summed = (
-        lax.psum(part_query.astype(jnp.bfloat16), "rep").astype(jnp.float32),
+        jnp.sum(lax.all_gather(part_query.astype(jnp.bfloat16), "rep"), axis=0).astype(jnp.float32),
         lax.psum(part_key.astype(jnp.bfloat16), "rep").astype(jnp.float32),
         lax.psum(part_value.astype(jnp.bfloat16), "rep").astype(jnp.float32),
         lax.psum(part_out.astype(jnp.bfloat16), "rep").astype(jnp.float32),

time: 740 us -> 729 us (0.985)
  blocking collectives: 79.9 us -> 92.5 us
  waiting for transfers between devices: 421 us -> 412 us
  local copies, waits for them, and re-layouts: 73.4 us -> 64.8 us
    reduce_scatter x0 -> x1, waiting for transfers between devices: none -> 29.7 us  [body(): lax.psum_scatter(grad_query_proj.astype(jnp.bfloat16), 'shard', scatter_d...]
    unnamed x19 -> x18, waiting for transfers between devices: 135 us -> 110 us
    all_gather x0 -> x1, blocking collectives: none -> 12.4 us  [body(): lax.all_gather(part_query.astype(jnp.bfloat16), 'rep')]
    psum x1, waiting for transfers between devices: 20.3 us -> 8.31 us  [body(): lax.psum(part_key.astype(jnp.bfloat16), 'rep').astype(jnp.float32)]
    unnamed x92 -> x114, local copies, waits for them, and re-layouts: 44.5 us -> 37.5 us
  transfers between devices with their start and end apart: 15 -> 15, of which waited for: 13 -> 13; matrix products, arithmetic and copies ran while one was open for 18% -> 17% of each run, Pallas kernels for 0% -> 0%
where the time goes in v1:
time: 729 us; the launch traced here: 727 us
  waiting for transfers between devices  412 us (57%)
  blocking collectives  92.5 us (13%)
  matrix products  92.1 us (13%)
  local copies, waits for them, and re-layouts  64.8 us (9%)
  other arithmetic  46.6 us (6%)
  between operations  17.3 us (2%)
    unnamed x18, waiting for transfers between devices  110 us
    all_gather x1, waiting for transfers between devices, body(): lax.all_gather(jnp.concatenate([keys, values], axis=1), 'shard', axis=0,...  58 us
    unnamed x2, blocking collectives  56.8 us
    reduce_scatter x1, waiting for transfers between devices, body(): lax.psum_scatter(grad_down.astype(jnp.bfloat16), 'shard', scatter_dimensi...  55.7 us
    reduce_scatter x1, waiting for transfers between devices, body(): lax.psum_scatter(grad_up.astype(jnp.bfloat16), 'shard', scatter_dimension...  55.3 us
    all_gather x1, waiting for transfers between devices, body(): lax.all_gather(w_down, 'shard', axis=0, tiled=True)  46.1 us
    unnamed x114, local copies, waits for them, and re-layouts  37.5 us
    reduce_scatter x1, waiting for transfers between devices, body(): lax.psum_scatter(grad_out_proj.astype(jnp.bfloat16), 'shard', scatter_dim...  31.8 us
  transfers between devices with their start and end apart: 15, of which 13 were waited for; matrix products, arithmetic and copies ran while one was open for 17% of the time, Pallas kernels for 0%

profile of v1, /device:TPU:0, one launch (start us, length us, event | category | flops | bytes accessed | tf_op | source)
XLA Modules:
  0.0 727.1 jit_solution(18072201837707202081)
XLA Ops:
  17.3 30.8 %all-reduce.18 = (bf16[768]{0:T(1024)(128)(2,1)S(1)}, bf16[768]{0:T(1024)(128)(2,1)S(1)}, bf16[768]{0:T(1024)(128)(2,1)S(1)}, bf16[768]{0:T(1024)(128)(2,1)S(1)}...) all-reduce(bf16[768]{0:T(1024)(128)(2,1)S(1)} %dynamic-update-slice, ...), channel_id=1, replica_groups=mesh['rep'=4,'shard'=8] {'shard'}, use_global_device_ids=true, to_apply=%add | all-reduce | flops 5376 | bytes 21504
  50.0 9.5 %all-gather.12.cloned.1.call-done = bf16[768,768]{1,0:T(8,128)(2,1)} async-done(((bf16[96,768]{1,0:T(8,128)(2,1)}), bf16[768,768]{1,0:T(8,128)(2,1)}) %all-gather.12.cloned.1.call-update) | async-done | bytes 1179664 | tf_op jit(solution)/shard_map/all_gather | solution.py:83
  64.8 12.9 %all-gather.1 = bf16[8,1,384]{2,1,0:T(2,128)(2,1)S(1)} all-gather(bf16[1,1,384]{2,1,0:T(2,128)(2,1)S(1)} %reshape.199), channel_id=1, replica_groups=mesh['rep'=4,'shard'=8] {'shard'}, dimensions={0}, use_global_device_ids=true | all-gather | bytes 6912 | tf_op jit(solution)/shard_map/all_gather | solution.py:91
  85.5 58.0 %all-gather.14.cloned.1.call-done = bf16[1792,1536]{1,0:T(8,128)(2,1)} async-done(((bf16[224,1536]{1,0:T(8,128)(2,1)}), bf16[1792,1536]{1,0:T(8,128)(2,1)}) %all-gather.14.cloned.1.call-update) | async-done | bytes 5505040 | tf_op jit(solution)/shard_map/all_gather | solution.py:130
  143.5 8.0 %copy.54 = bf16[1792,1536]{0,1:T(8,128)(2,1)} copy(bf16[1792,1536]{1,0:T(8,128)(2,1)} %all-gather.14.cloned.1.call-done) | data formatting | bytes 11010048
  151.6 25.5 %while.46 = (s32[]{:T(128)}, f32[12,224]{1,0:T(8,128)S(1)}, f32[12,224]{1,0:T(8,128)S(1)}, s32[]{:T(128)}, bf16[1792,1536]{0,1:T(8,128)(2,1)}, /*index=5*/bf16[2...) while((s32[]{:T(128)}, f32[12,224]{1,0:T(8,128)S(1)}, ...), condition=%wide.region_3.4_spmd.clone, body=%wide.region_0.3_spmd.clone.sunk | while | flops 93599368 | bytes 7169450 | solution.py:157
  177.1 34.2 %while.47 = (s32[]{:T(128)}, f32[224,12,64]{0,2,1:T(8,128)}, bf16[1792,1536]{0,1:T(8,128)(2,1)}, s32[]{:T(128)}, bf16[224,12,64]{0,2,1:T(8,128)(2,1)S(1)}, /*ind...) while((s32[]{:T(128)}, f32[224,12,64]{0,2,1:T(8,128)}, ...), condition=%wide.region_5.6_spmd.clone, body=%wide.region_4.5_spmd.clone.sunk | while | flops 179257856 | bytes 4091073 | solution.py:171
  218.9 5.6 multiply_convert_fusion.1
  224.5 46.1 %all-gather.22.cloned.1.call-done = bf16[3072,768]{1,0:T(8,128)(2,1)} async-done(((bf16[384,768]{1,0:T(8,128)(2,1)}), bf16[3072,768]{1,0:T(8,128)(2,1)}) %all-gather.22.cloned.1.call-update) | async-done | bytes 4718608 | tf_op jit(solution)/shard_map/all_gather | solution.py:92
  286.8 44.6 %while.48 = (s32[]{:T(128)}, f32[224,12,64]{0,2,1:T(8,128)S(1)}, bf16[1792,1536]{0,1:T(8,128)(2,1)}, bf16[1792,1536]{0,1:T(8,128)(2,1)}, s32[]{:T(128)}, /*index...) while((s32[]{:T(128)}, f32[224,12,64]{0,2,1:T(8,128)S(1)}, ...), condition=%wide.region_15.16_spmd.clone, body=%wide.region_14.15_spmd.clone.sunk | while | flops 449765888 | bytes 21660152 | solution.py:254
  331.4 8.3 %copy.68 = bf16[1792,1536]{1,0:T(8,128)(2,1)} copy(bf16[1792,1536]{0,1:T(8,128)(2,1)} %get-tuple-element.395) | data formatting | bytes 11010048
  339.7 61.2 %reduce-scatter.22.cloned.1.call-done = bf16[224,1536]{1,0:T(8,128)(2,1)} async-done(((bf16[1792,1536]{1,0:T(8,128)(2,1)}), bf16[224,1536]{1,0:T(8,128)(2,1)}) %reduce-scatter.22.cloned.1.call-update) | async-done | bytes 688144
  408.7 5.0 convolution_convert_fusion.1
  414.8 4.9 convolution_convert_fusion
  422.0 13.4 %reduce-scatter.26.cloned.1.call-done = bf16[96,768]{1,0:T(8,128)(2,1)} async-done(((bf16[768,768]{1,0:T(8,128)(2,1)}), bf16[96,768]{1,0:T(8,128)(2,1)}) %reduce-scatter.26.cloned.1.call-update) | async-done | bytes 147472
  437.2 31.6 %reduce-scatter.28.cloned.1.call-done = bf16[96,768]{1,0:T(8,128)(2,1)} async-done(((bf16[768,768]{1,0:T(8,128)(2,1)}), bf16[96,768]{1,0:T(8,128)(2,1)}) %reduce-scatter.28.cloned.1.call-update) | async-done | bytes 147472
  470.5 31.8 %reduce-scatter.16.cloned.1.call-done = bf16[96,768]{1,0:T(8,128)(2,1)} async-done(((bf16[768,768]{1,0:T(8,128)(2,1)}), bf16[96,768]{1,0:T(8,128)(2,1)}) %reduce-scatter.16.cloned.1.call-update) | async-done | bytes 147472 | tf_op jit(solution)/shard_map/reduce_scatter | solution.py:293
  502.3 55.3 %reduce-scatter.18.cloned.1.call-done = bf16[96,3072]{1,0:T(8,128)(2,1)} async-done(((bf16[768,3072]{1,0:T(8,128)(2,1)}), bf16[96,3072]{1,0:T(8,128)(2,1)}) %reduce-scatter.18.cloned.1.call-update) | async-done | bytes 589840 | tf_op jit(solution)/shard_map/reduce_scatter | solution.py:311
  557.6 55.7 %reduce-scatter.20.cloned.1.call-done = bf16[384,768]{1,0:T(8,128)(2,1)} async-done(((bf16[3072,768]{1,0:T(8,128)(2,1)}), bf16[384,768]{1,0:T(8,128)(2,1)}) %reduce-scatter.20.cloned.1.call-update) | async-done | bytes 589840 | tf_op jit(solution)/shard_map/reduce_scatter | solution.py:317
  617.8 29.7 %reduce-scatter.24.cloned.1.call-done = bf16[96,768]{1,0:T(8,128)(2,1)} async-done(((bf16[768,768]{1,0:T(8,128)(2,1)}), bf16[96,768]{1,0:T(8,128)(2,1)}) %reduce-scatter.24.cloned.1.call-update) | async-done | bytes 147472 | tf_op jit(solution)/shard_map/reduce_scatter | solution.py:284
  647.5 12.4 %all-gather = bf16[384,768]{1,0:T(8,128)(2,1)S(1)} all-gather(bf16[96,768]{1,0:T(8,128)(2,1)} %reduce-scatter.24.cloned.1.call-done), channel_id=2, replica_groups=mesh['rep'=4,'shard'=8] {'rep'}, dimensions={0}, use_global_device_ids=true | all-gather | bytes 737280 | tf_op jit(solution)/shard_map/all_gather | solution.py:348
  660.8 26.0 %all-reduce.17 = (bf16[768]{0:T(1024)(128)(2,1)S(1)}, bf16[768]{0:T(1024)(128)(2,1)S(1)}, bf16[768]{0:T(1024)(128)(2,1)S(1)}, bf16[768]{0:T(1024)(128)(2,1)S(1)}...) all-reduce(bf16[768]{0:T(1024)(128)(2,1)S(1)} %dynamic-update-slice, ...), channel_id=1, replica_groups=mesh['rep'=4,'shard'=8] {'shard'}, use_global_device_ids=true, to_apply=%add.7 | all-reduce | flops 9984 | bytes 39936
  687.5 10.4 %all-reduce.19 = (bf16[96]{0:T(256)(128)(2,1)S(1)}, bf16[96]{0:T(256)(128)(2,1)S(1)}, bf16[96]{0:T(256)(128)(2,1)S(1)}, bf16[96]{0:T(256)(128)(2,1)S(1)}, bf16[9...) all-reduce(bf16[96]{0:T(256)(128)(2,1)S(1)} %dynamic-slice.9, ...), channel_id=1, replica_groups=mesh['rep'=4,'shard'=8] {'rep'}, use_global_device_ids=true, to_apply=%region_27.28 | all-reduce | flops 1152 | bytes 4608 | tf_op jit(solution)/shard_map/psum | solution.py:352
  705.5 8.3 %all-reduce.23.cloned.1.call-done = (bf16[96,768]{0,1:T(8,128)(2,1)}, bf16[96,768]{0,1:T(8,128)(2,1)}, bf16[96,768]{1,0:T(8,128)(2,1)}, bf16[96,3072]{1,0:T(8,128)(2,1)}, bf16[384,768]{1,0:T(8,128)(2,1)}) async-done(((bf16[96,768]{0,1:T(8,128)(2,1)}, bf16[96,768]{0,1:T(8,128)(2,1)}, bf16[96,768]{1,0:T(8,128)(2,1)}, bf16[96,3072]{1,0:T(8,128)(2,1)}, bf16[384,768]{1,0:T(8,128)(2,1)}), ...) | async-done | bytes 1622032 | tf_op jit(solution)/shard_map/psum | solution.py:349
  (354 shorter events, 183.9 us)
Async XLA Ops:
  7.2 41.0 %all-gather.10.cloned.1.call-start = ((), (), s32[]{:S(2)}) async-start(), calls=%async_computation.7 | async-start | bytes 1327104 | tf_op jit(solution)/shard_map/all_gather | solution.py:82
  7.9 51.5 %all-gather.12.cloned.1.call-start = ((), (), s32[]{:S(2)}) async-start(), calls=%async_computation.8 | async-start | bytes 1327104 | tf_op jit(solution)/shard_map/all_gather | solution.py:83
  8.7 74.9 %all-gather.16.cloned.1.call-start = ((), (), s32[]{:S(2)}) async-start(), calls=%async_computation.10 | async-start | bytes 1327104 | tf_op jit(solution)/shard_map/all_gather | solution.py:81
  9.4 134.1 %all-gather.14.cloned.1.call-start = ((), (), s32[]{:S(2)}) async-start(), calls=%async_computation.9 | async-start | bytes 6193152 | tf_op jit(solution)/shard_map/all_gather | solution.py:130
  62.2 150.3 %all-gather.18.cloned.1.call-start = ((), (), s32[]{:S(2)}) async-start(), calls=%async_computation.11 | async-start | bytes 1327104 | tf_op jit(solution)/shard_map/all_gather | solution.py:84
  62.8 156.2 %all-gather.20.cloned.1.call-start = ((), (), s32[]{:S(2)}) async-start(), calls=%async_computation.12 | async-start | bytes 5308416 | tf_op jit(solution)/shard_map/all_gather | solution.py:90
  63.4 207.2 %all-gather.22.cloned.1.call-start = ((), (), s32[]{:S(2)}) async-start(), calls=%async_computation.13 | async-start | bytes 5308416 | tf_op jit(solution)/shard_map/all_gather | solution.py:92
  64.1 336.8 %reduce-scatter.22.cloned.1.call-start = ((), (), s32[]{:S(2)}) async-start(), calls=%async_computation.17 | async-start | bytes 6193152
  214.5 67.0 %copy-start.1 = (f32[224,768]{1,0:T(8,128)}, f32[224,768]{1,0:T(8,128)S(1)}, u32[]{:S(2)}) copy-start(f32[224,768]{1,0:T(8,128)S(1)} %get-tuple-element.678) | copy-start | bytes 2064388
  218.9 51.6 %copy-start.30 = (f32[768]{0:T(1024)S(1)}, f32[768]{0:T(1024)}, u32[]{:S(2)}) copy-start(f32[768]{0:T(1024)} %convert_element_type.255) | copy-start | bytes 9220
  224.5 49.9 %copy-start.13 = (bf16[224,3072]{1,0:T(8,128)(2,1)}, bf16[224,3072]{1,0:T(8,128)(2,1)S(1)}, u32[]{:S(2)}) copy-start(bf16[224,3072]{1,0:T(8,128)(2,1)S(1)} %get-tuple-element.679) | copy-start | bytes 4128772
  339.7 95.8 %reduce-scatter.26.cloned.1.call-start = ((), (), s32[]{:S(2)}) async-start(), calls=%async_computation.19 | async-start | bytes 1327104
  403.9 64.9 %reduce-scatter.28.cloned.1.call-start = ((), (), s32[]{:S(2)}) async-start(), calls=%async_computation.20 | async-start | bytes 1327104
  407.1 95.2 %reduce-scatter.16.cloned.1.call-start = ((), (), s32[]{:S(2)}) async-start(), calls=%async_computation.14 | async-start | bytes 1327104 | tf_op jit(solution)/shard_map/reduce_scatter | solution.py:293
  408.6 149.0 %reduce-scatter.18.cloned.1.call-start = ((), (), s32[]{:S(2)}) async-start(), calls=%async_computation.15 | async-start | bytes 5308416 | tf_op jit(solution)/shard_map/reduce_scatter | solution.py:311
  413.7 199.6 %reduce-scatter.20.cloned.1.call-start = ((), (), s32[]{:S(2)}) async-start(), calls=%async_computation.16 | async-start | bytes 5308416 | tf_op jit(solution)/shard_map/reduce_scatter | solution.py:317
  419.8 227.7 %reduce-scatter.24.cloned.1.call-start = ((), (), s32[]{:S(2)}) async-start(), calls=%async_computation.18 | async-start | bytes 1327104 | tf_op jit(solution)/shard_map/reduce_scatter | solution.py:284
  420.5 194.3 %copy-start.34 = (bf16[96]{0:T(256)(128)(2,1)S(1)}, bf16[96]{0:T(256)(128)(2,1)}, u32[]{:S(2)}) copy-start(bf16[96]{0:T(256)(128)(2,1)} %param.41) | copy-start | bytes 580
  422.0 291.8 %all-reduce.23.cloned.1.call-start = ((), (), s32[]{:S(2)}) async-start(), calls=%async_computation.21 | async-start | bytes 3440640 | tf_op jit(solution)/shard_map/psum | solution.py:349
  613.3 47.4 %copy-start.29 = (bf16[3072]{0:T(1024)(128)(2,1)S(1)}, bf16[3072]{0:T(1024)(128)(2,1)}, u32[]{:S(2)}) copy-start(bf16[3072]{0:T(1024)(128)(2,1)} %get-tuple-element.684) | copy-start | bytes 18436
  613.4 47.4 %copy-start.31 = (bf16[768]{0:T(1024)(128)(2,1)S(1)}, bf16[768]{0:T(1024)(128)(2,1)}, u32[]{:S(2)}) copy-start(bf16[768]{0:T(1024)(128)(2,1)} %get-tuple-element.582) | copy-start | bytes 4612
  613.4 47.4 %copy-start.32 = (bf16[768]{0:T(1024)(128)(2,1)S(1)}, bf16[768]{0:T(1024)(128)(2,1)}, u32[]{:S(2)}) copy-start(bf16[768]{0:T(1024)(128)(2,1)} %get-tuple-element.587) | copy-start | bytes 4612
  613.4 89.2 %copy-start.8 = (bf16[768,768]{1,0:T(8,128)(2,1)S(1)}, bf16[768,768]{1,0:T(8,128)(2,1)}, u32[]{:S(2)}) copy-start(bf16[768,768]{1,0:T(8,128)(2,1)} %all-gather.10.cloned.1.call-done) | copy-start | bytes 3538948
  617.8 84.8 %copy-start.15 = (f32[224,768]{1,0:T(8,128)S(1)}, f32[224,768]{1,0:T(8,128)}, u32[]{:S(2)}) copy-start(f32[224,768]{1,0:T(8,128)} %convolution_add_fusion.3) | copy-start | bytes 2064388
  (37 other events, 243.5 us)
Sparse Core Ops, SparseCore 0:
  9.6 25.6 all-gather.9
  36.9 22.4 all-gather.11
  61.1 22.4 all-gather.15
  85.7 57.7 all-gather.13
  145.0 21.5 all-gather.17
  168.1 50.8 all-gather.19
  220.6 49.9 all-gather.21
  339.8 61.0 reduce-scatter.21
  404.0 31.3 reduce-scatter.25
  437.6 31.1 reduce-scatter.27
  471.1 31.1 reduce-scatter.15
  504.5 53.1 reduce-scatter.17
  559.9 53.3 reduce-scatter.19
  616.0 31.4 reduce-scatter.23
  651.6 62.0 all-reduce.22
